TPU v7x, 256 devices: a whole 4x4x8 slice. The times are simulated.
256 devices in a mesh: space: 8 (over z), work: 32 (over y, x, core).
Axes of the slice: x: 4, y: 4, z: 8, core: 2. Of those that a mesh axis runs over, the one named last changes fastest.
Arguments:
- positions: float32 [3, 262144], P(None, ('space', 'work')), may hold values from -3 to 3
- velocities: float32 [3, 262144], P(None, ('space', 'work')), may hold values from -2 to 2
- masses: float32 [262144], P(('space', 'work')), may hold values from 0.001 to 0.01
- sound2: float32 [262144], P(('space', 'work')), may hold values from 0.1 to 1
- ghost_list: int32 [1024, 2], P(('space', 'work')), may hold values from 0 to 7
- dens_list: int32 [2048, 6], P(('space', 'work')), may hold values from 0 to 15
- pair_dest: int32 [16384, 1], P(('space', 'work')), may hold values from 0 to 31; in each aligned block of 64 rows (0 to 63, 64 to 127, ...) at most 4 rows name the same one
- pair_tiles: int32 [16384, 2], P(('space', 'work')), may hold values from 0 to 7
Outputs:
- new_positions: float32 [3, 262144], P(None, ('space', 'work'))
- new_velocities: float32 [3, 262144], P(None, ('space', 'work'))
- acceleration: float32 [3, 262144], P(None, ('space', 'work'))
- density: float32 [262144], P(('space', 'work'))
Inputs may be any that keep to these rules, and one draw needn't show every extreme that they name: `pair_dest`: at most 4 pairs of one device name the same owner; in every draw some device has exactly 4 pairs for one owner.
All inputs are finite; a program needn't handle non-finite values.
Results may differ from a plain program's by a relative error of at most 0.0001.
Values sent between devices are 32-bit elements; how exact they have to be, the bound alone decides.
No kernel may reach another device: no remote copies, remote signals or barrier semaphores. Data moves between devices by JAX's collectives and lax.ppermute only.
A program may use at most 64 MiB of HBM per device.

v0:
```python
import jax
import jax.numpy as jnp
from jax import lax
from jax.experimental import pallas as pl
from jax.experimental.pallas import tpu as pltpu
from jax.sharding import Mesh, PartitionSpec as P

TD = 8
G = 4
NBD = 6
CAP = 4
PAIRS = 64
CHIPS = 16
OTHERS = 2 * CHIPS * TD
LOG2E = 1.4426950408889634
STAR = 0.5
SOFT = 0.1
DT = 0.1
SPAN = 512
GRANT = 16 * 1024 * 1024

VMEM = pl.BlockSpec(memory_space=pltpu.VMEM)
HBM = pl.BlockSpec(memory_space=pltpu.HBM)
SMEM = pl.BlockSpec(memory_space=pltpu.SMEM)


def f32(*shape):
    return jax.ShapeDtypeStruct(shape, jnp.float32)


def i32(*shape):
    return jax.ShapeDtypeStruct(shape, jnp.int32)


def begin_kernel(pos_in, vel_in, mass_in, sound2_in, ghost_in, lists_in, dest_in, tiles_in,
                 to_next, to_prev, codes, table, pos, vel, mass, sound2, ghost_out, lists,
                 wide_pos, wide_vel, dest, tiles, ghost, sems):
    moves = (
        (ghost_in, ghost),
        (pos_in, wide_pos),
        (mass_in, mass),
        (dest_in, dest),
        (tiles_in, tiles),
        (vel_in, wide_vel),
        (sound2_in, sound2),
        (lists_in, lists),
        (ghost_in, ghost_out),
    )
    copies = [pltpu.make_async_copy(src, dst, sems.at[n]) for n, (src, dst) in enumerate(moves)]
    for copy in copies:
        copy.start()
    for copy in copies:
        copy.wait()
    for t in range(TD):
        span = slice(128 * t, 128 * t + 128)
        for k in range(3):
            pos[8 * k + t : 8 * k + t + 1, :] = wide_pos[k : k + 1, span]
            vel[8 * k + t : 8 * k + t + 1, :] = wide_vel[k : k + 1, span]
    fill_outgoing(ghost, pos, mass, to_next, to_prev)
    core = lax.axis_index("core")
    d = dest[...]
    t0 = tiles[0:1, :]
    t1 = tiles[1:2, :]
    half = (d & 1) ^ core
    code = (t0 * SPAN + half * (CHIPS * TD) + (d >> 1) * TD + t1).astype(jnp.float32)
    row = lax.broadcasted_iota(jnp.int32, (PAIRS // CAP, PAIRS), 0)
    column = lax.broadcasted_iota(jnp.int32, (PAIRS // CAP, PAIRS), 1)
    lane = lax.broadcasted_iota(jnp.int32, (PAIRS // CAP, 128), 1)
    out = jnp.zeros((PAIRS // CAP, 128), jnp.float32)
    for c in range(CAP):
        chosen = jnp.where(column == CAP * row + c, code, 0.0)
        out = jnp.where(lane == c, jnp.sum(chosen, axis=1, keepdims=True), out)
    codes[...] = out.astype(jnp.int32)
    place = lax.broadcasted_iota(jnp.int32, (2 * CHIPS, PAIRS), 0)
    hits = (place == d).astype(jnp.float32)
    earlier = (
        lax.broadcasted_iota(jnp.int32, (PAIRS, PAIRS), 0)
        < lax.broadcasted_iota(jnp.int32, (PAIRS, PAIRS), 1)
    ).astype(jnp.float32)
    rank = jnp.dot(hits, earlier, preferred_element_type=jnp.float32)
    first = t0.astype(jnp.float32)
    second = t1.astype(jnp.float32) + 1.0
    lane = lax.broadcasted_iota(jnp.int32, (2 * CHIPS, 128), 1)
    out = jnp.zeros((2 * CHIPS, 128), jnp.float32)
    for c in range(CAP):
        chosen = jnp.where(rank == float(c), hits, 0.0)
        out = jnp.where(lane == c, jnp.sum(chosen * second, axis=1, keepdims=True), out)
        out = jnp.where(lane == CAP + c, jnp.sum(chosen * first, axis=1, keepdims=True), out)
    table[...] = out


def fill_outgoing(ghost, pos, mass, to_next, to_prev):
    for side, out in enumerate((to_next, to_prev)):
        for j in range(G):
            t = ghost[side, j]
            for k in range(3):
                out[4 * j + k : 4 * j + k + 1, :] = pos[pl.ds(8 * k + t, 1), :]
            out[4 * j + 3 : 4 * j + 4, :] = mass[pl.ds(t, 1), :]


def diagonal():
    sub = lax.broadcasted_iota(jnp.int32, (8, 128), 0)
    lane = lax.broadcasted_iota(jnp.int32, (8, 128), 1)
    return [lane == 8 * b + sub for b in range(16)]


def lane_sums(blocks, picks):
    total = jnp.zeros((8, 128), jnp.float32)
    for block, pick in zip(blocks, picks):
        total = jnp.where(pick, jnp.sum(block, axis=1, keepdims=True), total)
    return jnp.sum(total, axis=0, keepdims=True)


def spread_rows(rows, first, count, out):
    columns = jnp.transpose(rows[first : first + 128, :], (1, 0))
    for r in range(count):
        out[first + r] = jnp.broadcast_to(columns[:, r : r + 1], (128, 128))


def spread_kernel(pos, vel, own, rows):
    for t in range(TD):
        for k in range(3):
            rows[6 * t + k : 6 * t + k + 1, :] = pos[8 * k + t : 8 * k + t + 1, :]
            rows[6 * t + 3 + k : 6 * t + 4 + k, :] = vel[8 * k + t : 8 * k + t + 1, :]
    rows[48:128, :] = jnp.zeros((80, 128), jnp.float32)
    spread_rows(rows, 0, 48, own)


def density_of(cand, own, rho, lists):
    picks = diagonal()

    def one(t, carry):
        listed = [t] + [lists[t, c] for c in range(NBD)]
        other = [[cand[pl.ds(4 * j + k, 8, stride=0), :] for k in range(4)] for j in listed]
        blocks = []
        for b in range(16):
            rows = slice(8 * b, 8 * b + 8)
            xi, yi, zi = [own[6 * t + k, rows, :] for k in range(3)]
            total = None
            for xj, yj, zj, mj in other:
                dx = xi - xj
                dy = yi - yj
                dz = zi - zj
                part = jnp.exp2(mj - (dx * dx + dy * dy + dz * dz) * LOG2E)
                total = part if total is None else total + part
            blocks.append(total)
        rho[pl.ds(t, 1), :] = lane_sums(blocks, picks)
        return carry

    lax.fori_loop(0, TD, one, 0)


def fill_ghosts(cand, below, above):
    row = lax.broadcasted_iota(jnp.int32, (4 * G, 128), 0)
    for start, ref in ((4 * TD, below), (4 * TD + 4 * G, above)):
        value = ref[...]
        value = jnp.where(row % 4 == 3, jnp.log2(jnp.where(row % 4 == 3, value, 1.0)), value)
        cand[start : start + 4 * G, :] = value


def fill_candidates(cand, pos, heavy, below, above):
    for t in range(TD):
        for k in range(3):
            cand[4 * t + k : 4 * t + k + 1, :] = pos[8 * k + t : 8 * k + t + 1, :]
        cand[4 * t + 3 : 4 * t + 4, :] = heavy[t : t + 1, :]
    fill_ghosts(cand, below, above)


def density_first(pos, vel, mass, sound2, below, above, lists, table, own, sent, density, cand):
    heavy = jnp.log2(mass[...])
    fill_candidates(cand, pos, heavy, below, above)
    density_of(cand, own, density, lists)
    places = pos[...]
    speeds = vel[...]
    sound = 0.25 * jnp.sqrt(sound2[...])
    rho = density[...]
    for q in range(CHIPS):
        sent[q, 0:24, :] = places
        sent[q, 24:48, :] = speeds
        sent[q, 48:56, :] = heavy + 1.0
        sent[q, 56:64, :] = sound
        sent[q, 64:72, :] = rho
        sent[q, 72:80, :] = jnp.zeros((8, 128), jnp.float32)
        sent[q, 72:74, :] = table[2 * q : 2 * q + 2, :]


def density_second(pos, mass, accel, below, above, lists, own, sent, density, cand):
    fill_candidates(cand, pos, jnp.log2(mass[...]), below, above)
    density_of(cand, own, density, lists)
    moved = accel[...]
    rho = density[...]
    for q in range(CHIPS):
        sent[q, 0:24, :] = moved
        sent[q, 24:32, :] = rho


def pair_loop(listed, own, own_state, other, gains):
    for r in range(3 * TD):
        gains[r] = jnp.zeros((128, 128), jnp.float32)

    def force(code):
        t = code >> 9
        base = t * 6
        place = t * 3
        o = code & (SPAN - 1)
        xj, yj, zj, uj, vj, wj, sj, rj, pj, mj = [
            other[f, pl.ds(o, 8, stride=0), :] for f in range(10)
        ]
        for b in range(16):
            rows = slice(8 * b, 8 * b + 8)
            dx = own[base, rows, :] - xj
            dy = own[base + 1, rows, :] - yj
            dz = own[base + 2, rows, :] - zj
            d2 = dx * dx + dy * dy + dz * dz
            closing = (
                (own[base + 3, rows, :] - uj) * dx
                + (own[base + 4, rows, :] - vj) * dy
                + (own[base + 5, rows, :] - wj) * dz
            )
            closing = jnp.minimum(closing, 0.0)
            near = d2 + 0.01
            bottom = near * near * (own_state[place + 1, rows, :] + rj)
            guess = pl.reciprocal(bottom, approx=True)
            inverse = guess * (2.0 - bottom * guess)
            viscous = closing * (closing - (own_state[place, rows, :] + sj) * near) * inverse
            strength = own_state[place + 2, rows, :] + pj + viscous
            weight = strength * jnp.exp2(mj - d2 * LOG2E)
            gains[place, rows, :] += weight * dx
            gains[place + 1, rows, :] += weight * dy
            gains[place + 2, rows, :] += weight * dz

    def one(n, carry):
        for code in [listed[n, c] for c in range(CAP)]:
            force(code)
        return carry

    lax.fori_loop(0, PAIRS // CAP + 2 * CHIPS, one, 0)


def gathered_gain(gains, gain_rows):
    picks = diagonal()
    for t in range(TD):
        for k in range(3):
            blocks = [gains[3 * t + k, 8 * b : 8 * b + 8, :] for b in range(16)]
            gain_rows[8 * k + t : 8 * k + t + 1, :] = lane_sums(blocks, picks)


def fill_own_state(rows, own_state, sound2, rho):
    state = (0.25 * jnp.sqrt(sound2), 0.25 * rho, sound2 / rho)
    rows[3 * TD : 128, :] = jnp.zeros((128 - 3 * TD, 128), jnp.float32)
    for f, value in enumerate(state):
        for t in range(TD):
            rows[3 * t + f : 3 * t + f + 1, :] = value[t : t + 1, :]
    spread_rows(rows, 0, 3 * TD, own_state)


def fill_other(other, half, fields, sound, rho, heavy):
    spot = slice(half * CHIPS * TD, (half + 1) * CHIPS * TD)
    quarter = 0.25 * rho
    for f, value in enumerate(fields + [sound, quarter, 4.0 * sound * sound / quarter, heavy]):
        other[f, spot, :] = value.reshape(CHIPS * TD, 128)


def fill_dummy(other):
    for f in range(9):
        other[f, OTHERS : OTHERS + 8, :] = jnp.zeros((8, 128), jnp.float32)
    other[9, OTHERS : OTHERS + 8, :] = jnp.full((8, 128), -1e30, jnp.float32)


def listing(codes, mine, twin, hits, listed, sem):
    core = lax.axis_index("core")
    own_rows = PAIRS // CAP
    hits[0:own_rows, :] = codes[...]
    place = lax.broadcasted_iota(jnp.int32, (CHIPS, 128), 0)
    for half, ref in enumerate((mine, twin)):
        got = ref[:, 72:80, :]
        named = jnp.where(core == 0, got[:, 0, :], got[:, 1, :])
        first = pltpu.roll(named, 128 - CAP, 1)
        code = (named.astype(jnp.int32) - 1) * SPAN + (half * CHIPS + place) * TD
        code = code + first.astype(jnp.int32)
        start = own_rows + half * CHIPS
        hits[start : start + CHIPS, :] = jnp.where(named > 0.5, code, OTHERS)
    copy = pltpu.make_async_copy(hits, listed, sem)
    copy.start()
    return copy


def advance(gain_rows, xs, vs):
    radius2 = xs[0] * xs[0] + xs[1] * xs[1] + xs[2] * xs[2] + SOFT
    pull = -STAR / (radius2 * jnp.sqrt(radius2))
    accel = [gain_rows[8 * k : 8 * k + 8, :] + pull * xs[k] for k in range(3)]
    speed = [vs[k] + DT * accel[k] for k in range(3)]
    place = [xs[k] + DT * speed[k] for k in range(3)]
    return accel, speed, place


def pairs_first(mine, twin, codes, ghost, pos, vel, mass, sound2, rho, own,
                new_pos, new_vel, accel, to_next, to_prev,
                own_state, other, gains, rows, gain_rows, hits, listed, sem):
    copy = listing(codes, mine, twin, hits, listed, sem)
    xs = [pos[8 * k : 8 * k + 8, :] for k in range(3)]
    vs = [vel[8 * k : 8 * k + 8, :] for k in range(3)]
    fill_own_state(rows, own_state, sound2[...], rho[...])
    for half, ref in enumerate((mine, twin)):
        fields = [ref[:, 8 * f : 8 * f + 8, :] for f in range(9)]
        fill_other(other, half, fields[0:6], fields[7], fields[8], fields[6])
    fill_dummy(other)
    copy.wait()
    pair_loop(listed, own, own_state, other, gains)
    gathered_gain(gains, gain_rows)
    acc, speed, place = advance(gain_rows, xs, vs)
    for k in range(3):
        accel[8 * k : 8 * k + 8, :] = acc[k]
        new_vel[8 * k : 8 * k + 8, :] = speed[k]
        new_pos[8 * k : 8 * k + 8, :] = place[k]
    fill_outgoing(ghost, new_pos, mass, to_next, to_prev)


def pairs_second(mine, twin, mine_new, twin_new, codes, pos, vel, sound2, rho, own,
                 out_pos, out_vel, out_accel, out_rho,
                 own_state, other, gains, rows, gain_rows, hits, listed, sem):
    copy = listing(codes, mine, twin, hits, listed, sem)
    out_rho[...] = rho[...]
    fill_own_state(rows, own_state, sound2[...], rho[...])
    for half, (ref, new) in enumerate(((mine, mine_new), (twin, twin_new))):
        old = [ref[:, 8 * f : 8 * f + 8, :] for f in range(8)]
        speed = [old[3 + k] + DT * new[:, 8 * k : 8 * k + 8, :] for k in range(3)]
        place = [old[k] + DT * speed[k] for k in range(3)]
        fill_other(other, half, place + speed, old[7], new[:, 24:32, :], old[6])
    fill_dummy(other)
    copy.wait()
    pair_loop(listed, own, own_state, other, gains)
    gathered_gain(gains, gain_rows)
    xs = [pos[8 * k : 8 * k + 8, :] for k in range(3)]
    vs = [vel[8 * k : 8 * k + 8, :] for k in range(3)]
    acc, speed, place = advance(gain_rows, xs, vs)
    for k in range(3):
        for t in range(TD):
            span = slice(128 * t, 128 * t + 128)
            out_accel[k : k + 1, span] = acc[k][t : t + 1, :]
            out_vel[k : k + 1, span] = speed[k][t : t + 1, :]
            out_pos[k : k + 1, span] = place[k][t : t + 1, :]


def call(kernel, outs, ins, scratch=(), name=None):
    specs = [{"s": SMEM, "v": VMEM, "h": HBM}[spec] for spec in ins]
    return pl.pallas_call(
        kernel,
        out_shape=outs,
        in_specs=specs,
        out_specs=jax.tree.map(lambda _: VMEM, outs),
        scratch_shapes=scratch,
        compiler_params=pltpu.CompilerParams(vmem_limit_bytes=GRANT),
        name=name,
    )


def along_space(value, steps):
    count = lax.axis_size("space")
    return lax.ppermute(value, "space", [(i, (i + steps) % count) for i in range(count)])


def sector(value):
    mine = lax.all_to_all(value, "chip", 0, 0, tiled=True)
    return mine, lax.ppermute(mine, "core", [(0, 1), (1, 0)])


def local(positions, velocities, masses, sound2, ghost_list, dens_list, pair_dest, pair_tiles):
    pair_scratch = [
        pltpu.VMEM((3 * TD, 128, 128), jnp.float32),
        pltpu.VMEM((10, OTHERS + 8, 128), jnp.float32),
        pltpu.VMEM((3 * TD, 128, 128), jnp.float32),
        pltpu.VMEM((128, 128), jnp.float32),
        pltpu.VMEM((3 * TD, 128), jnp.float32),
        pltpu.VMEM((PAIRS // CAP + 2 * CHIPS, 128), jnp.int32),
        pltpu.SMEM((PAIRS // CAP + 2 * CHIPS, 128), jnp.int32),
        pltpu.SemaphoreType.DMA,
    ]
    cand = [pltpu.VMEM((4 * (TD + 2 * G) + 8, 128), jnp.float32)]
    spread = [pltpu.VMEM((128, 128), jnp.float32)]
    ghost_rows = f32(4 * G, 128)
    spread_shape = f32(6 * TD, 128, 128)
    to_next, to_prev, codes, table, pos, vel, mass, snd, ghost, lists = call(
        begin_kernel,
        (
            ghost_rows,
            ghost_rows,
            i32(PAIRS // CAP, 128),
            f32(2 * CHIPS, 128),
            f32(24, 128),
            f32(24, 128),
            f32(TD, 128),
            f32(TD, 128),
            i32(2, G),
            i32(TD, NBD),
        ),
        "hhhhhhhh",
        scratch=[
            pltpu.VMEM((3, 128 * TD), jnp.float32),
            pltpu.VMEM((3, 128 * TD), jnp.float32),
            pltpu.VMEM((1, PAIRS), jnp.int32),
            pltpu.VMEM((2, PAIRS), jnp.int32),
            pltpu.SMEM((2, G), jnp.int32),
            pltpu.SemaphoreType.DMA((9,)),
        ],
        name="begin",
    )(
        *(
            pltpu.with_memory_space_constraint(value, pltpu.HBM)
            for value in (
                positions,
                velocities,
                masses.reshape(TD, 128),
                sound2.reshape(TD, 128),
                ghost_list.T,
                dens_list,
                pair_dest.T,
                pair_tiles.T,
            )
        )
    )
    below = along_space(to_next, 1)
    above = along_space(to_prev, -1)
    own = call(spread_kernel, spread_shape, "vv", scratch=spread, name="spread_first")(pos, vel)
    sent, rho = call(
        density_first,
        (f32(CHIPS, 80, 128), f32(TD, 128)),
        "vvvvvvsvv",
        scratch=cand,
        name="density_first",
    )(pos, vel, mass, snd, below, above, lists, table, own)
    mine, twin = sector(sent)
    new_pos, new_vel, accel, to_next, to_prev = call(
        pairs_first,
        (f32(24, 128), f32(24, 128), f32(24, 128), ghost_rows, ghost_rows),
        "vvvsvvvvvv",
        scratch=pair_scratch,
        name="pairs_first",
    )(mine, twin, codes, ghost, pos, vel, mass, snd, rho, own)
    below = along_space(to_next, 1)
    above = along_space(to_prev, -1)
    own = call(spread_kernel, spread_shape, "vv", scratch=spread, name="spread_second")(
        new_pos, new_vel
    )
    sent, rho = call(
        density_second,
        (f32(CHIPS, 32, 128), f32(TD, 128)),
        "vvvvvsv",
        scratch=cand,
        name="density_second",
    )(new_pos, mass, accel, below, above, lists, own)
    mine_new, twin_new = sector(sent)
    out_pos, out_vel, out_accel, out_rho = call(
        pairs_second,
        (f32(3, 1024), f32(3, 1024), f32(3, 1024), f32(TD, 128)),
        "vvvvvvvvvv",
        scratch=pair_scratch,
        name="pairs_second",
    )(mine, twin, mine_new, twin_new, codes, new_pos, new_vel, snd, rho, own)
    return (out_pos, out_vel, out_accel, out_rho.reshape(TD * 128))


def solution(mesh):
    grid = Mesh(mesh.devices.reshape(mesh.devices.shape[0], CHIPS, 2), ("space", "chip", "core"))
    every = ("space", "chip", "core")
    return jax.shard_map(
        local,
        mesh=grid,
        in_specs=(
            P(None, every),
            P(None, every),
            P(every),
            P(every),
            P(every, None),
            P(every, None),
            P(every, None),
            P(every, None),
        ),
        out_specs=(P(None, every), P(None, every), P(None, every), P(every)),
        check_vma=False,
    )
```

profile of v0, /device:TPU:1, one launch (start us, length us, event | category | flops | bytes accessed | tf_op | source)
XLA Modules:
  0.0 97.9 jit_solution(14358431432517335543)
XLA Ops:
  0.6 1.1 %begin.1 = (f32[16,128]{1,0:T(8,128)S(1)}, f32[16,128]{1,0:T(8,128)S(1)}, s32[16,128]{1,0:T(8,128)S(1)}, f32[32,128]{1,0:T(8,128)S(1)}, f32[24,128]{1,0:T(8,128)...) custom-call(f32[3,1024]{1,0:T(4,128)} %pos_in.1, ...), custom_call_target="tpu_custom_call" | custom-call | tf_op jit(solution)/shard_map/begin/pallas_call | solution.py:383
  1.8 2.5 %collective-permute-start = (f32[16,128]{1,0:T(8,128)S(1)}, f32[16,128]{1,0:T(8,128)S(1)}, u32[]{:S(2)}, u32[]{:S(2)}) collective-permute-start(f32[16,128]{1,0:T(8,128)S(1)} %get-tuple-element.31), channel_id=1, source_target_pairs={{0,32},{32,64},{64,96},{96,128},{128,160},{160,192},{192,224},{224... | collective-permute-start | bytes 24584 | tf_op jit(solution)/shard_map/ppermute | solution.py:360
  4.3 4.0 %collective-permute-start.1 = (f32[16,128]{1,0:T(8,128)S(1)}, f32[16,128]{1,0:T(8,128)S(1)}, u32[]{:S(2)}, u32[]{:S(2)}) collective-permute-start(f32[16,128]{1,0:T(8,128)S(1)} %get-tuple-element.32), channel_id=1, source_target_pairs={{0,224},{32,0},{64,32},{96,64},{128,96},{160,128},{192,160},{224,1... | collective-permute-start | bytes 24584 | tf_op jit(solution)/shard_map/ppermute | solution.py:360
  8.3 1.1 %spread_first.1.own = f32[48,128,128]{2,1,0:T(8,128)S(1)} custom-call(f32[24,128]{1,0:T(8,128)S(1)} %get-tuple-element.27.pos, f32[24,128]{1,0:T(8,128)S(1)} %get-tuple-element.28.vel), custom_call_target="tpu_custom_call" | custom-call | tf_op jit(solution)/shard_map/spread_first/pallas_call | solution.py:424
  9.4 0.0 collective-permute-done.below
  9.4 0.0 collective-permute-done.1.above
  9.4 2.8 %density_first.1 = (f32[16,80,128]{2,1,0:T(8,128)S(1)}, f32[8,128]{1,0:T(8,128)S(1)}) custom-call(f32[24,128]{1,0:T(8,128)S(1)} %get-tuple-element.27.pos, f32[24,128]{1,0:T(8,128)S(1)} %get-tuple-element.28.vel, f32[8,128]{1,0:T(8,128)S(1)} %get-tuple-element.29.mass, f32[8,128]{1,0:T(8,128)S(1)} %get-tuple-element.30.sound2, ...), custom_call_target="tpu_custom_call" | custom-call | tf_op jit(solution)/shard_map/density_first/pallas_call | solution.py:425
  12.2 18.0 %all_to_all.10.mine = f32[16,80,128]{2,1,0:T(8,128)S(1)} all-to-all(f32[16,80,128]{2,1,0:T(8,128)S(1)} %get-tuple-element.35), channel_id=1, replica_groups=mesh['space'=8,'chip'=16,'core'=2] {'chip'}, dimensions={0} | all-to-all | bytes 1310720 | tf_op jit(solution)/shard_map/all_to_all | solution.py:364
  30.2 2.5 %collective-permute-start.2 = (f32[16,80,128]{2,1,0:T(8,128)S(1)}, f32[16,80,128]{2,1,0:T(8,128)S(1)}, u32[]{:S(2)}, u32[]{:S(2)}) collective-permute-start(f32[16,80,128]{2,1,0:T(8,128)S(1)} %all_to_all.10.mine), channel_id=1, source_target_pairs={{0,1},{1,0},{2,3},{3,2},{4,5},{5,4},{6,7},{7,6},{8,9},{9,8},{10,11... | collective-permute-start | bytes 1966088 | tf_op jit(solution)/shard_map/ppermute | solution.py:365
  32.7 1.7 %collective-permute-done.2.twin = f32[16,80,128]{2,1,0:T(8,128)S(1)} collective-permute-done((f32[16,80,128]{2,1,0:T(8,128)S(1)}, f32[16,80,128]{2,1,0:T(8,128)S(1)}, u32[]{:S(2)}, u32[]{:S(2)}) %collective-permute-start.2) | collective-permute-done | bytes 655392 | tf_op jit(solution)/shard_map/ppermute | solution.py:365
  34.4 21.1 %pairs_first.1 = (f32[24,128]{1,0:T(8,128)S(1)}, f32[24,128]{1,0:T(8,128)S(1)}, f32[24,128]{1,0:T(8,128)S(1)}, f32[16,128]{1,0:T(8,128)S(1)}, f32[16,128]{1,0:T(8,128)S(1)}) custom-call(f32[16,80,128]{2,1,0:T(8,128)S(1)} %all_to_all.10.mine, f32[16,80,128]{2,1,0:T(8,128)S(1)} %collective-permute-done.2.twin, s32[16,128]{1,0:T(8,128)S(1)} %get-tuple-element.36.codes, ...), custom_call_target="tpu_custom_call" | custom-call | tf_op jit(solution)/shard_map/pairs_first/pallas_call | solution.py:433
  55.5 0.1 collective-permute-start.3
  55.6 2.7 %collective-permute-start.4 = (f32[16,128]{1,0:T(8,128)S(1)}, f32[16,128]{1,0:T(8,128)S(1)}, u32[]{:S(2)}, u32[]{:S(2)}) collective-permute-start(f32[16,128]{1,0:T(8,128)S(1)} %get-tuple-element.42), channel_id=1, source_target_pairs={{0,224},{32,0},{64,32},{96,64},{128,96},{160,128},{192,160},{224,1... | collective-permute-start | bytes 24584 | tf_op jit(solution)/shard_map/ppermute | solution.py:360
  58.3 1.1 %spread_second.1.own = f32[48,128,128]{2,1,0:T(8,128)S(1)} custom-call(f32[24,128]{1,0:T(8,128)S(1)} %get-tuple-element.39.pos, f32[24,128]{1,0:T(8,128)S(1)} %get-tuple-element.43.vel), custom_call_target="tpu_custom_call" | custom-call | tf_op jit(solution)/shard_map/spread_second/pallas_call | solution.py:442
  59.4 0.0 collective-permute-done.3.below
  59.4 0.0 collective-permute-done.4.above
  59.4 2.8 %density_second.1 = (f32[16,32,128]{2,1,0:T(8,128)S(1)}, f32[8,128]{1,0:T(8,128)S(1)}) custom-call(f32[24,128]{1,0:T(8,128)S(1)} %get-tuple-element.39.pos, f32[8,128]{1,0:T(8,128)S(1)} %get-tuple-element.29.mass, f32[24,128]{1,0:T(8,128)S(1)} %get-tuple-element.40.accel, f32[16,128]{1,0:T(8,128)S(1)} %collective-permute-done.3.below, ...), custom_call_target="tpu_custom_call" | custom-call | tf_op jit(solution)/shard_map/density_second/pallas_call | solution.py:445
  62.2 10.5 %all_to_all.11.mine_new = f32[16,32,128]{2,1,0:T(8,128)S(1)} all-to-all(f32[16,32,128]{2,1,0:T(8,128)S(1)} %get-tuple-element.44), channel_id=1, replica_groups=mesh['space'=8,'chip'=16,'core'=2] {'chip'}, dimensions={0} | all-to-all | bytes 524288 | tf_op jit(solution)/shard_map/all_to_all | solution.py:364
  72.7 2.7 %collective-permute-start.5 = (f32[16,32,128]{2,1,0:T(8,128)S(1)}, f32[16,32,128]{2,1,0:T(8,128)S(1)}, u32[]{:S(2)}, u32[]{:S(2)}) collective-permute-start(f32[16,32,128]{2,1,0:T(8,128)S(1)} %all_to_all.11.mine_new), channel_id=1, source_target_pairs={{0,1},{1,0},{2,3},{3,2},{4,5},{5,4},{6,7},{7,6},{8,9},{9,8},{10,11... | collective-permute-start | bytes 786440 | tf_op jit(solution)/shard_map/ppermute | solution.py:365
  75.5 1.2 %collective-permute-done.5.twin_new = f32[16,32,128]{2,1,0:T(8,128)S(1)} collective-permute-done((f32[16,32,128]{2,1,0:T(8,128)S(1)}, f32[16,32,128]{2,1,0:T(8,128)S(1)}, u32[]{:S(2)}, u32[]{:S(2)}) %collective-permute-start.5) | collective-permute-done | bytes 262176 | tf_op jit(solution)/shard_map/ppermute | solution.py:365
  76.6 21.3 %pairs_second.1 = (f32[3,1024]{1,0:T(4,128)}, f32[3,1024]{1,0:T(4,128)}, f32[3,1024]{1,0:T(4,128)}, f32[8,128]{1,0:T(8,128)}) custom-call(f32[16,80,128]{2,1,0:T(8,128)S(1)} %all_to_all.10.mine, f32[16,80,128]{2,1,0:T(8,128)S(1)} %collective-permute-done.2.twin, f32[16,32,128]{2,1,0:T(8,128)S(1)} %all_to_all.11.mine_new, ...), custom_call_target="tpu_custom_call" | custom-call | tf_op jit(solution)/shard_map/pairs_second/pallas_call | solution.py:453
Async XLA Ops:
  1.8 7.6 %collective-permute-start = (f32[16,128]{1,0:T(8,128)S(1)}, f32[16,128]{1,0:T(8,128)S(1)}, u32[]{:S(2)}, u32[]{:S(2)}) collective-permute-start(f32[16,128]{1,0:T(8,128)S(1)} %get-tuple-element.31), channel_id=1, source_target_pairs={{0,32},{32,64},{64,96},{96,128},{128,160},{160,192},{192,224},{224... | collective-permute-start | bytes 24584 | tf_op jit(solution)/shard_map/ppermute | solution.py:360
  4.3 5.1 %collective-permute-start.1 = (f32[16,128]{1,0:T(8,128)S(1)}, f32[16,128]{1,0:T(8,128)S(1)}, u32[]{:S(2)}, u32[]{:S(2)}) collective-permute-start(f32[16,128]{1,0:T(8,128)S(1)} %get-tuple-element.32), channel_id=1, source_target_pairs={{0,224},{32,0},{64,32},{96,64},{128,96},{160,128},{192,160},{224,1... | collective-permute-start | bytes 24584 | tf_op jit(solution)/shard_map/ppermute | solution.py:360
  30.2 4.2 %collective-permute-start.2 = (f32[16,80,128]{2,1,0:T(8,128)S(1)}, f32[16,80,128]{2,1,0:T(8,128)S(1)}, u32[]{:S(2)}, u32[]{:S(2)}) collective-permute-start(f32[16,80,128]{2,1,0:T(8,128)S(1)} %all_to_all.10.mine), channel_id=1, source_target_pairs={{0,1},{1,0},{2,3},{3,2},{4,5},{5,4},{6,7},{7,6},{8,9},{9,8},{10,11... | collective-permute-start | bytes 1966088 | tf_op jit(solution)/shard_map/ppermute | solution.py:365
  55.5 3.9 %collective-permute-start.3 = (f32[16,128]{1,0:T(8,128)S(1)}, f32[16,128]{1,0:T(8,128)S(1)}, u32[]{:S(2)}, u32[]{:S(2)}) collective-permute-start(f32[16,128]{1,0:T(8,128)S(1)} %get-tuple-element.41), channel_id=1, source_target_pairs={{0,32},{32,64},{64,96},{96,128},{128,160},{160,192},{192,224},{224... | collective-permute-start | bytes 24584 | tf_op jit(solution)/shard_map/ppermute | solution.py:360
  55.6 3.8 %collective-permute-start.4 = (f32[16,128]{1,0:T(8,128)S(1)}, f32[16,128]{1,0:T(8,128)S(1)}, u32[]{:S(2)}, u32[]{:S(2)}) collective-permute-start(f32[16,128]{1,0:T(8,128)S(1)} %get-tuple-element.42), channel_id=1, source_target_pairs={{0,224},{32,0},{64,32},{96,64},{128,96},{160,128},{192,160},{224,1... | collective-permute-start | bytes 24584 | tf_op jit(solution)/shard_map/ppermute | solution.py:360
  72.7 3.9 %collective-permute-start.5 = (f32[16,32,128]{2,1,0:T(8,128)S(1)}, f32[16,32,128]{2,1,0:T(8,128)S(1)}, u32[]{:S(2)}, u32[]{:S(2)}) collective-permute-start(f32[16,32,128]{2,1,0:T(8,128)S(1)} %all_to_all.11.mine_new), channel_id=1, source_target_pairs={{0,1},{1,0},{2,3},{3,2},{4,5},{5,4},{6,7},{7,6},{8,9},{9,8},{10,11... | collective-permute-start | bytes 786440 | tf_op jit(solution)/shard_map/ppermute | solution.py:365
where the time goes:
time: 98.1 us; the launch traced here: 97.9 us
  Pallas kernels  51.3 us (52%)
  blocking collectives  28.5 us (29%)
  starting transfers between devices  14.6 us (15%)
  waiting for transfers between devices  2.9 us (3%)
    all_to_all x2, blocking collectives, sector(): mine = lax.all_to_all(value, 'chip', 0, 0, tiled=True)  28.5 us
    pallas_call x1, Pallas kernels, local(): call(pairs_second, (f32(3, 1024), f32(3, 1024), f32(3, 1024), f32(TD, 128...  21.3 us
    pallas_call x1, Pallas kernels, local(): call(pairs_first, (f32(24, 128), f32(24, 128), f32(24, 128), ghost_rows,...  21.1 us
    ppermute x4, starting transfers between devices, along_space(): lax.ppermute(value, 'space', [(i, (i + steps) % count) for i in range(cou...  9.36 us
    ppermute x2, starting transfers between devices, sector(): return (mine, lax.ppermute(mine, 'core', [(0, 1), (1, 0)]))  5.21 us
    ppermute x2, waiting for transfers between devices, sector(): return (mine, lax.ppermute(mine, 'core', [(0, 1), (1, 0)]))  2.89 us
    pallas_call x1, Pallas kernels, local(): call(density_first, (f32(CHIPS, 80, 128), f32(TD, 128)), 'vvvvvvsvv', scr...  2.8 us
    pallas_call x1, Pallas kernels, local(): call(density_second, (f32(CHIPS, 32, 128), f32(TD, 128)), 'vvvvvsv', scra...  2.8 us
  transfers between devices with their start and end apart: 6, of which 2 were waited for; matrix products, arithmetic and copies ran while one was open for 0% of the time, Pallas kernels for 2%

commit v1 on v0

--- a/solution.py
+++ b/solution.py
@@ -1,3 +1,5 @@
+import math
+
 import jax
 import jax.numpy as jnp
 from jax import lax
@@ -13,10 +15,12 @@
 CHIPS = 16
 OTHERS = 2 * CHIPS * TD
 LOG2E = 1.4426950408889634
+ROOT = LOG2E**0.5
 STAR = 0.5
 SOFT = 0.1
 DT = 0.1
 SPAN = 512
+UNROLL = 8
 GRANT = 16 * 1024 * 1024
 
 VMEM = pl.BlockSpec(memory_space=pltpu.VMEM)
@@ -111,19 +115,27 @@
     return jnp.sum(total, axis=0, keepdims=True)
 
 
-def spread_rows(rows, first, count, out):
-    columns = jnp.transpose(rows[first : first + 128, :], (1, 0))
-    for r in range(count):
-        out[first + r] = jnp.broadcast_to(columns[:, r : r + 1], (128, 128))
-
-
-def spread_kernel(pos, vel, own, rows):
-    for t in range(TD):
-        for k in range(3):
-            rows[6 * t + k : 6 * t + k + 1, :] = pos[8 * k + t : 8 * k + t + 1, :]
-            rows[6 * t + 3 + k : 6 * t + 4 + k, :] = vel[8 * k + t : 8 * k + t + 1, :]
-    rows[48:128, :] = jnp.zeros((80, 128), jnp.float32)
-    spread_rows(rows, 0, 48, own)
+def spread_places(pos, own, rows):
+    spread_tiles([pos[8 * k : 8 * k + 8, :] * ROOT for k in range(3)], own, rows)
+
+
+def spread_rest(vel, sound2, rho, own, rows):
+    fields = [vel[8 * k : 8 * k + 8, :] for k in range(3)]
+    square = sound2[...]
+    dense = rho[...]
+    fields += [0.25 / ROOT * jnp.sqrt(square), 0.25 / LOG2E * dense, square / dense]
+    spread_tiles(fields, own, rows)
+
+
+def spread_tiles(fields, own, rows):
+    count = len(fields)
+    for f, value in enumerate(fields):
+        for t in range(TD):
+            rows[count * t + f : count * t + f + 1, :] = value[t : t + 1, :]
+    rows[count * TD : 128, :] = jnp.zeros((128 - count * TD, 128), jnp.float32)
+    columns = jnp.transpose(rows[...], (1, 0))
+    for r in range(count * TD):
+        own[r] = jnp.broadcast_to(columns[:, r : r + 1], (128, 128))
 
 
 def density_of(cand, own, rho, lists):
@@ -135,13 +147,13 @@
         blocks = []
         for b in range(16):
             rows = slice(8 * b, 8 * b + 8)
-            xi, yi, zi = [own[6 * t + k, rows, :] for k in range(3)]
+            xi, yi, zi = [own[3 * t + k, rows, :] for k in range(3)]
             total = None
             for xj, yj, zj, mj in other:
                 dx = xi - xj
                 dy = yi - yj
                 dz = zi - zj
-                part = jnp.exp2(mj - (dx * dx + dy * dy + dz * dz) * LOG2E)
+                part = jnp.exp2(mj - (dx * dx + dy * dy + dz * dz))
                 total = part if total is None else total + part
             blocks.append(total)
         rho[pl.ds(t, 1), :] = lane_sums(blocks, picks)
@@ -154,14 +166,14 @@
     row = lax.broadcasted_iota(jnp.int32, (4 * G, 128), 0)
     for start, ref in ((4 * TD, below), (4 * TD + 4 * G, above)):
         value = ref[...]
-        value = jnp.where(row % 4 == 3, jnp.log2(jnp.where(row % 4 == 3, value, 1.0)), value)
+        value = jnp.where(row % 4 == 3, jnp.log2(jnp.where(row % 4 == 3, value, 1.0)), value * ROOT)
         cand[start : start + 4 * G, :] = value
 
 
 def fill_candidates(cand, pos, heavy, below, above):
     for t in range(TD):
         for k in range(3):
-            cand[4 * t + k : 4 * t + k + 1, :] = pos[8 * k + t : 8 * k + t + 1, :]
+            cand[4 * t + k : 4 * t + k + 1, :] = pos[8 * k + t : 8 * k + t + 1, :] * ROOT
         cand[4 * t + 3 : 4 * t + 4, :] = heavy[t : t + 1, :]
     fill_ghosts(cand, below, above)
 
@@ -172,12 +184,12 @@
     density_of(cand, own, density, lists)
     places = pos[...]
     speeds = vel[...]
-    sound = 0.25 * jnp.sqrt(sound2[...])
+    sound = 0.25 / ROOT * jnp.sqrt(sound2[...])
     rho = density[...]
     for q in range(CHIPS):
         sent[q, 0:24, :] = places
         sent[q, 24:48, :] = speeds
-        sent[q, 48:56, :] = heavy + 1.0
+        sent[q, 48:56, :] = heavy + (1.0 - math.log2(ROOT))
         sent[q, 56:64, :] = sound
         sent[q, 64:72, :] = rho
         sent[q, 72:80, :] = jnp.zeros((8, 128), jnp.float32)
@@ -194,47 +206,45 @@
         sent[q, 24:32, :] = rho
 
 
-def pair_loop(listed, own, own_state, other, gains):
+def pair_loop(listed, own, own_rest, other, gains):
     for r in range(3 * TD):
         gains[r] = jnp.zeros((128, 128), jnp.float32)
 
     def force(code):
         t = code >> 9
-        base = t * 6
         place = t * 3
+        rest = t * 6
         o = code & (SPAN - 1)
         xj, yj, zj, uj, vj, wj, sj, rj, pj, mj = [
             other[f, pl.ds(o, 8, stride=0), :] for f in range(10)
         ]
         for b in range(16):
             rows = slice(8 * b, 8 * b + 8)
-            dx = own[base, rows, :] - xj
-            dy = own[base + 1, rows, :] - yj
-            dz = own[base + 2, rows, :] - zj
+            dx = own[place, rows, :] - xj
+            dy = own[place + 1, rows, :] - yj
+            dz = own[place + 2, rows, :] - zj
             d2 = dx * dx + dy * dy + dz * dz
             closing = (
-                (own[base + 3, rows, :] - uj) * dx
-                + (own[base + 4, rows, :] - vj) * dy
-                + (own[base + 5, rows, :] - wj) * dz
+                (own_rest[rest, rows, :] - uj) * dx
+                + (own_rest[rest + 1, rows, :] - vj) * dy
+                + (own_rest[rest + 2, rows, :] - wj) * dz
             )
             closing = jnp.minimum(closing, 0.0)
-            near = d2 + 0.01
-            bottom = near * near * (own_state[place + 1, rows, :] + rj)
-            guess = pl.reciprocal(bottom, approx=True)
-            inverse = guess * (2.0 - bottom * guess)
-            viscous = closing * (closing - (own_state[place, rows, :] + sj) * near) * inverse
-            strength = own_state[place + 2, rows, :] + pj + viscous
-            weight = strength * jnp.exp2(mj - d2 * LOG2E)
+            near = d2 + 0.01 * LOG2E
+            bottom = near * near * (own_rest[rest + 4, rows, :] + rj)
+            viscous = closing * (closing - (own_rest[rest + 3, rows, :] + sj) * near) / bottom
+            strength = own_rest[rest + 5, rows, :] + pj + viscous
+            weight = strength * jnp.exp2(mj - d2)
             gains[place, rows, :] += weight * dx
             gains[place + 1, rows, :] += weight * dy
             gains[place + 2, rows, :] += weight * dz
 
     def one(n, carry):
-        for code in [listed[n, c] for c in range(CAP)]:
-            force(code)
+        for u in range(UNROLL):
+            force(listed[(UNROLL // CAP) * n + u // CAP, u % CAP])
         return carry
 
-    lax.fori_loop(0, PAIRS // CAP + 2 * CHIPS, one, 0)
+    lax.fori_loop(0, (PAIRS + 2 * CHIPS * CAP) // UNROLL, one, 0)
 
 
 def gathered_gain(gains, gain_rows):
@@ -245,19 +255,11 @@
             gain_rows[8 * k + t : 8 * k + t + 1, :] = lane_sums(blocks, picks)
 
 
-def fill_own_state(rows, own_state, sound2, rho):
-    state = (0.25 * jnp.sqrt(sound2), 0.25 * rho, sound2 / rho)
-    rows[3 * TD : 128, :] = jnp.zeros((128 - 3 * TD, 128), jnp.float32)
-    for f, value in enumerate(state):
-        for t in range(TD):
-            rows[3 * t + f : 3 * t + f + 1, :] = value[t : t + 1, :]
-    spread_rows(rows, 0, 3 * TD, own_state)
-
-
 def fill_other(other, half, fields, sound, rho, heavy):
     spot = slice(half * CHIPS * TD, (half + 1) * CHIPS * TD)
-    quarter = 0.25 * rho
-    for f, value in enumerate(fields + [sound, quarter, 4.0 * sound * sound / quarter, heavy]):
+    pressure = 16.0 * LOG2E * sound * sound / rho
+    fields = [ROOT * x for x in fields[0:3]] + list(fields[3:6])
+    for f, value in enumerate(fields + [sound, 0.25 / LOG2E * rho, pressure, heavy]):
         other[f, spot, :] = value.reshape(CHIPS * TD, 128)
 
 
@@ -294,19 +296,18 @@
     return accel, speed, place
 
 
-def pairs_first(mine, twin, codes, ghost, pos, vel, mass, sound2, rho, own,
+def pairs_first(mine, twin, codes, ghost, pos, vel, mass, own, own_rest,
                 new_pos, new_vel, accel, to_next, to_prev,
-                own_state, other, gains, rows, gain_rows, hits, listed, sem):
+                other, gains, gain_rows, hits, listed, sem):
     copy = listing(codes, mine, twin, hits, listed, sem)
     xs = [pos[8 * k : 8 * k + 8, :] for k in range(3)]
     vs = [vel[8 * k : 8 * k + 8, :] for k in range(3)]
-    fill_own_state(rows, own_state, sound2[...], rho[...])
     for half, ref in enumerate((mine, twin)):
         fields = [ref[:, 8 * f : 8 * f + 8, :] for f in range(9)]
         fill_other(other, half, fields[0:6], fields[7], fields[8], fields[6])
     fill_dummy(other)
     copy.wait()
-    pair_loop(listed, own, own_state, other, gains)
+    pair_loop(listed, own, own_rest, other, gains)
     gathered_gain(gains, gain_rows)
     acc, speed, place = advance(gain_rows, xs, vs)
     for k in range(3):
@@ -316,12 +317,11 @@
     fill_outgoing(ghost, new_pos, mass, to_next, to_prev)
 
 
-def pairs_second(mine, twin, mine_new, twin_new, codes, pos, vel, sound2, rho, own,
+def pairs_second(mine, twin, mine_new, twin_new, codes, pos, vel, rho, own, own_rest,
                  out_pos, out_vel, out_accel, out_rho,
-                 own_state, other, gains, rows, gain_rows, hits, listed, sem):
+                 other, gains, gain_rows, hits, listed, sem):
     copy = listing(codes, mine, twin, hits, listed, sem)
     out_rho[...] = rho[...]
-    fill_own_state(rows, own_state, sound2[...], rho[...])
     for half, (ref, new) in enumerate(((mine, mine_new), (twin, twin_new))):
         old = [ref[:, 8 * f : 8 * f + 8, :] for f in range(8)]
         speed = [old[3 + k] + DT * new[:, 8 * k : 8 * k + 8, :] for k in range(3)]
@@ -329,7 +329,7 @@
         fill_other(other, half, place + speed, old[7], new[:, 24:32, :], old[6])
     fill_dummy(other)
     copy.wait()
-    pair_loop(listed, own, own_state, other, gains)
+    pair_loop(listed, own, own_rest, other, gains)
     gathered_gain(gains, gain_rows)
     xs = [pos[8 * k : 8 * k + 8, :] for k in range(3)]
     vs = [vel[8 * k : 8 * k + 8, :] for k in range(3)]
@@ -367,10 +367,8 @@
 
 def local(positions, velocities, masses, sound2, ghost_list, dens_list, pair_dest, pair_tiles):
     pair_scratch = [
-        pltpu.VMEM((3 * TD, 128, 128), jnp.float32),
         pltpu.VMEM((10, OTHERS + 8, 128), jnp.float32),
         pltpu.VMEM((3 * TD, 128, 128), jnp.float32),
-        pltpu.VMEM((128, 128), jnp.float32),
         pltpu.VMEM((3 * TD, 128), jnp.float32),
         pltpu.VMEM((PAIRS // CAP + 2 * CHIPS, 128), jnp.int32),
         pltpu.SMEM((PAIRS // CAP + 2 * CHIPS, 128), jnp.int32),
@@ -379,7 +377,8 @@
     cand = [pltpu.VMEM((4 * (TD + 2 * G) + 8, 128), jnp.float32)]
     spread = [pltpu.VMEM((128, 128), jnp.float32)]
     ghost_rows = f32(4 * G, 128)
-    spread_shape = f32(6 * TD, 128, 128)
+    places_shape = f32(3 * TD, 128, 128)
+    rest_shape = f32(6 * TD, 128, 128)
     to_next, to_prev, codes, table, pos, vel, mass, snd, ghost, lists = call(
         begin_kernel,
         (
@@ -421,7 +420,7 @@
     )
     below = along_space(to_next, 1)
     above = along_space(to_prev, -1)
-    own = call(spread_kernel, spread_shape, "vv", scratch=spread, name="spread_first")(pos, vel)
+    own = call(spread_places, places_shape, "v", scratch=spread, name="places_first")(pos)
     sent, rho = call(
         density_first,
         (f32(CHIPS, 80, 128), f32(TD, 128)),
@@ -430,18 +429,17 @@
         name="density_first",
     )(pos, vel, mass, snd, below, above, lists, table, own)
     mine, twin = sector(sent)
+    rest = call(spread_rest, rest_shape, "vvv", scratch=spread, name="rest_first")(vel, snd, rho)
     new_pos, new_vel, accel, to_next, to_prev = call(
         pairs_first,
         (f32(24, 128), f32(24, 128), f32(24, 128), ghost_rows, ghost_rows),
-        "vvvsvvvvvv",
+        "vvvsvvvvv",
         scratch=pair_scratch,
         name="pairs_first",
-    )(mine, twin, codes, ghost, pos, vel, mass, snd, rho, own)
+    )(mine, twin, codes, ghost, pos, vel, mass, own, rest)
     below = along_space(to_next, 1)
     above = along_space(to_prev, -1)
-    own = call(spread_kernel, spread_shape, "vv", scratch=spread, name="spread_second")(
-        new_pos, new_vel
-    )
+    own = call(spread_places, places_shape, "v", scratch=spread, name="places_second")(new_pos)
     sent, rho = call(
         density_second,
         (f32(CHIPS, 32, 128), f32(TD, 128)),
@@ -450,13 +448,16 @@
         name="density_second",
     )(new_pos, mass, accel, below, above, lists, own)
     mine_new, twin_new = sector(sent)
+    rest = call(spread_rest, rest_shape, "vvv", scratch=spread, name="rest_second")(
+        new_vel, snd, rho
+    )
     out_pos, out_vel, out_accel, out_rho = call(
         pairs_second,
         (f32(3, 1024), f32(3, 1024), f32(3, 1024), f32(TD, 128)),
         "vvvvvvvvvv",
         scratch=pair_scratch,
         name="pairs_second",
-    )(mine, twin, mine_new, twin_new, codes, new_pos, new_vel, snd, rho, own)
+    )(mine, twin, mine_new, twin_new, codes, new_pos, new_vel, rho, own, rest)
     return (out_pos, out_vel, out_accel, out_rho.reshape(TD * 128))
 
 

time: 98.1 us -> 92.6 us (0.944)
  Pallas kernels: 51.3 us -> 47 us
  waiting for transfers between devices: 2.9 us -> 1.38 us
    pallas_call x1, Pallas kernels: 21.3 us -> 18.6 us  [local(): call(pairs_second, (f32(3, 1024), f32(3, 1024), f32(3, 1024), f32(TD, 128...]
    pallas_call x1, Pallas kernels: 21.1 us -> 18.5 us  [local(): call(pairs_first, (f32(24, 128), f32(24, 128), f32(24, 128), ghost_rows,...]
    ppermute x2, waiting for transfers between devices: 2.89 us -> 0.73 us  [sector(): return (mine, lax.ppermute(mine, 'core', [(0, 1), (1, 0)]))]
    pallas_call x2 -> x4, Pallas kernels: 2.14 us -> 3.38 us  [the longest x1 1.07 us: local(): call(spread_rest, rest_shape, 'vvv', scratch=spread, name='rest_first')]
  transfers between devices with their start and end apart: 6 -> 6, of which waited for: 2 -> 4; matrix products, arithmetic and copies ran while one was open for 0% -> 0% of each run, Pallas kernels for 2% -> 4%
where the time goes in v1:
time: 92.6 us; the launch traced here: 92.3 us
  Pallas kernels  47 us (51%)
  blocking collectives  28.4 us (31%)
  starting transfers between devices  14.8 us (16%)
  waiting for transfers between devices  1.38 us (1%)
    all_to_all x2, blocking collectives, sector(): mine = lax.all_to_all(value, 'chip', 0, 0, tiled=True)  28.4 us
    pallas_call x1, Pallas kernels, local(): call(pairs_second, (f32(3, 1024), f32(3, 1024), f32(3, 1024), f32(TD, 128...  18.6 us
    pallas_call x1, Pallas kernels, local(): call(pairs_first, (f32(24, 128), f32(24, 128), f32(24, 128), ghost_rows,...  18.5 us
    ppermute x4, starting transfers between devices, along_space(): lax.ppermute(value, 'space', [(i, (i + steps) % count) for i in range(cou...  9.47 us
    ppermute x2, starting transfers between devices, sector(): return (mine, lax.ppermute(mine, 'core', [(0, 1), (1, 0)]))  5.36 us
    pallas_call x1, Pallas kernels, local(): call(density_first, (f32(CHIPS, 80, 128), f32(TD, 128)), 'vvvvvvsvv', scr...  2.69 us
    pallas_call x1, Pallas kernels, local(): call(density_second, (f32(CHIPS, 32, 128), f32(TD, 128)), 'vvvvvsv', scra...  2.68 us
  transfers between devices with their start and end apart: 6, of which 4 were waited for; matrix products, arithmetic and copies ran while one was open for 0% of the time, Pallas kernels for 4%

profile of v1, /device:TPU:1, one launch (start us, length us, event | category | flops | bytes accessed | tf_op | source)
XLA Modules:
  0.0 92.3 jit_solution(5065609834157081056)
XLA Ops:
  0.6 1.1 %begin.1 = (f32[16,128]{1,0:T(8,128)S(1)}, f32[16,128]{1,0:T(8,128)S(1)}, s32[16,128]{1,0:T(8,128)S(1)}, f32[32,128]{1,0:T(8,128)S(1)}, f32[24,128]{1,0:T(8,128)...) custom-call(f32[3,1024]{1,0:T(4,128)} %pos_in.1, ...), custom_call_target="tpu_custom_call" | custom-call | tf_op jit(solution)/shard_map/begin/pallas_call | solution.py:382
  1.8 2.5 %collective-permute-start = (f32[16,128]{1,0:T(8,128)S(1)}, f32[16,128]{1,0:T(8,128)S(1)}, u32[]{:S(2)}, u32[]{:S(2)}) collective-permute-start(f32[16,128]{1,0:T(8,128)S(1)} %get-tuple-element.31), channel_id=1, source_target_pairs={{0,32},{32,64},{64,96},{96,128},{128,160},{160,192},{192,224},{224... | collective-permute-start | bytes 24584 | tf_op jit(solution)/shard_map/ppermute | solution.py:360
  4.3 4.0 %collective-permute-start.1 = (f32[16,128]{1,0:T(8,128)S(1)}, f32[16,128]{1,0:T(8,128)S(1)}, u32[]{:S(2)}, u32[]{:S(2)}) collective-permute-start(f32[16,128]{1,0:T(8,128)S(1)} %get-tuple-element.32), channel_id=1, source_target_pairs={{0,224},{32,0},{64,32},{96,64},{128,96},{160,128},{192,160},{224,1... | collective-permute-start | bytes 24584 | tf_op jit(solution)/shard_map/ppermute | solution.py:360
  8.3 0.6 places_first.1.own
  9.0 0.3 collective-permute-done.below
  9.3 0.0 collective-permute-done.1.above
  9.3 2.7 %density_first.1 = (f32[16,80,128]{2,1,0:T(8,128)S(1)}, f32[8,128]{1,0:T(8,128)S(1)}) custom-call(f32[24,128]{1,0:T(8,128)S(1)} %get-tuple-element.27.pos, f32[24,128]{1,0:T(8,128)S(1)} %get-tuple-element.28.vel, f32[8,128]{1,0:T(8,128)S(1)} %get-tuple-element.29.mass, f32[8,128]{1,0:T(8,128)S(1)} %get-tuple-element.30.sound2, ...), custom_call_target="tpu_custom_call" | custom-call | tf_op jit(solution)/shard_map/density_first/pallas_call | solution.py:424
  12.0 17.9 %all_to_all.10.mine = f32[16,80,128]{2,1,0:T(8,128)S(1)} all-to-all(f32[16,80,128]{2,1,0:T(8,128)S(1)} %get-tuple-element.35), channel_id=1, replica_groups=mesh['space'=8,'chip'=16,'core'=2] {'chip'}, dimensions={0} | all-to-all | bytes 1310720 | tf_op jit(solution)/shard_map/all_to_all | solution.py:364
  29.8 2.6 %collective-permute-start.2 = (f32[16,80,128]{2,1,0:T(8,128)S(1)}, f32[16,80,128]{2,1,0:T(8,128)S(1)}, u32[]{:S(2)}, u32[]{:S(2)}) collective-permute-start(f32[16,80,128]{2,1,0:T(8,128)S(1)} %all_to_all.10.mine), channel_id=1, source_target_pairs={{0,1},{1,0},{2,3},{3,2},{4,5},{5,4},{6,7},{7,6},{8,9},{9,8},{10,11... | collective-permute-start | bytes 1966088 | tf_op jit(solution)/shard_map/ppermute | solution.py:365
  32.5 1.1 %rest_first.1.own_rest = f32[48,128,128]{2,1,0:T(8,128)S(1)} custom-call(f32[24,128]{1,0:T(8,128)S(1)} %get-tuple-element.28.vel, f32[8,128]{1,0:T(8,128)S(1)} %get-tuple-element.30.sound2, f32[8,128]{1,0:T(8,128)S(1)} %get-tuple-element.38.rho), custom_call_target="tpu_custom_call" | custom-call | tf_op jit(solution)/shard_map/rest_first/pallas_call | solution.py:432
  33.6 0.6 collective-permute-done.2.twin
  34.2 18.5 %pairs_first.1 = (f32[24,128]{1,0:T(8,128)S(1)}, f32[24,128]{1,0:T(8,128)S(1)}, f32[24,128]{1,0:T(8,128)S(1)}, f32[16,128]{1,0:T(8,128)S(1)}, f32[16,128]{1,0:T(8,128)S(1)}) custom-call(f32[16,80,128]{2,1,0:T(8,128)S(1)} %all_to_all.10.mine, f32[16,80,128]{2,1,0:T(8,128)S(1)} %collective-permute-done.2.twin, s32[16,128]{1,0:T(8,128)S(1)} %get-tuple-element.36.codes, ...), custom_call_target="tpu_custom_call" | custom-call | tf_op jit(solution)/shard_map/pairs_first/pallas_call | solution.py:433
  52.7 0.1 collective-permute-start.3
  52.8 2.8 %collective-permute-start.4 = (f32[16,128]{1,0:T(8,128)S(1)}, f32[16,128]{1,0:T(8,128)S(1)}, u32[]{:S(2)}, u32[]{:S(2)}) collective-permute-start(f32[16,128]{1,0:T(8,128)S(1)} %get-tuple-element.42), channel_id=1, source_target_pairs={{0,224},{32,0},{64,32},{96,64},{128,96},{160,128},{192,160},{224,1... | collective-permute-start | bytes 24584 | tf_op jit(solution)/shard_map/ppermute | solution.py:360
  55.7 0.6 places_second.1.own
  56.3 0.3 collective-permute-done.3.below
  56.6 0.0 collective-permute-done.4.above
  56.6 2.7 %density_second.1 = (f32[16,32,128]{2,1,0:T(8,128)S(1)}, f32[8,128]{1,0:T(8,128)S(1)}) custom-call(f32[24,128]{1,0:T(8,128)S(1)} %get-tuple-element.39.pos, f32[8,128]{1,0:T(8,128)S(1)} %get-tuple-element.29.mass, f32[24,128]{1,0:T(8,128)S(1)} %get-tuple-element.40.accel, f32[16,128]{1,0:T(8,128)S(1)} %collective-permute-done.3.below, ...), custom_call_target="tpu_custom_call" | custom-call | tf_op jit(solution)/shard_map/density_second/pallas_call | solution.py:443
  59.3 10.6 %all_to_all.11.mine_new = f32[16,32,128]{2,1,0:T(8,128)S(1)} all-to-all(f32[16,32,128]{2,1,0:T(8,128)S(1)} %get-tuple-element.43), channel_id=1, replica_groups=mesh['space'=8,'chip'=16,'core'=2] {'chip'}, dimensions={0} | all-to-all | bytes 524288 | tf_op jit(solution)/shard_map/all_to_all | solution.py:364
  69.9 2.7 %collective-permute-start.5 = (f32[16,32,128]{2,1,0:T(8,128)S(1)}, f32[16,32,128]{2,1,0:T(8,128)S(1)}, u32[]{:S(2)}, u32[]{:S(2)}) collective-permute-start(f32[16,32,128]{2,1,0:T(8,128)S(1)} %all_to_all.11.mine_new), channel_id=1, source_target_pairs={{0,1},{1,0},{2,3},{3,2},{4,5},{5,4},{6,7},{7,6},{8,9},{9,8},{10,11... | collective-permute-start | bytes 786440 | tf_op jit(solution)/shard_map/ppermute | solution.py:365
  72.6 1.1 %rest_second.1.own_rest = f32[48,128,128]{2,1,0:T(8,128)S(1)} custom-call(f32[24,128]{1,0:T(8,128)S(1)} %get-tuple-element.44.vel, f32[8,128]{1,0:T(8,128)S(1)} %get-tuple-element.30.sound2, f32[8,128]{1,0:T(8,128)S(1)} %get-tuple-element.45.rho), custom_call_target="tpu_custom_call" | custom-call | tf_op jit(solution)/shard_map/rest_second/pallas_call | solution.py:451
  73.7 0.1 collective-permute-done.5.twin_new
  73.8 18.6 %pairs_second.1 = (f32[3,1024]{1,0:T(4,128)}, f32[3,1024]{1,0:T(4,128)}, f32[3,1024]{1,0:T(4,128)}, f32[8,128]{1,0:T(8,128)}) custom-call(f32[16,80,128]{2,1,0:T(8,128)S(1)} %all_to_all.10.mine, f32[16,80,128]{2,1,0:T(8,128)S(1)} %collective-permute-done.2.twin, f32[16,32,128]{2,1,0:T(8,128)S(1)} %all_to_all.11.mine_new, ...), custom_call_target="tpu_custom_call" | custom-call | tf_op jit(solution)/shard_map/pairs_second/pallas_call | solution.py:454
Async XLA Ops:
  1.8 7.5 %collective-permute-start = (f32[16,128]{1,0:T(8,128)S(1)}, f32[16,128]{1,0:T(8,128)S(1)}, u32[]{:S(2)}, u32[]{:S(2)}) collective-permute-start(f32[16,128]{1,0:T(8,128)S(1)} %get-tuple-element.31), channel_id=1, source_target_pairs={{0,32},{32,64},{64,96},{96,128},{128,160},{160,192},{192,224},{224... | collective-permute-start | bytes 24584 | tf_op jit(solution)/shard_map/ppermute | solution.py:360
  4.3 5.0 %collective-permute-start.1 = (f32[16,128]{1,0:T(8,128)S(1)}, f32[16,128]{1,0:T(8,128)S(1)}, u32[]{:S(2)}, u32[]{:S(2)}) collective-permute-start(f32[16,128]{1,0:T(8,128)S(1)} %get-tuple-element.32), channel_id=1, source_target_pairs={{0,224},{32,0},{64,32},{96,64},{128,96},{160,128},{192,160},{224,1... | collective-permute-start | bytes 24584 | tf_op jit(solution)/shard_map/ppermute | solution.py:360
  29.8 4.4 %collective-permute-start.2 = (f32[16,80,128]{2,1,0:T(8,128)S(1)}, f32[16,80,128]{2,1,0:T(8,128)S(1)}, u32[]{:S(2)}, u32[]{:S(2)}) collective-permute-start(f32[16,80,128]{2,1,0:T(8,128)S(1)} %all_to_all.10.mine), channel_id=1, source_target_pairs={{0,1},{1,0},{2,3},{3,2},{4,5},{5,4},{6,7},{7,6},{8,9},{9,8},{10,11... | collective-permute-start | bytes 1966088 | tf_op jit(solution)/shard_map/ppermute | solution.py:365
  52.7 3.9 %collective-permute-start.3 = (f32[16,128]{1,0:T(8,128)S(1)}, f32[16,128]{1,0:T(8,128)S(1)}, u32[]{:S(2)}, u32[]{:S(2)}) collective-permute-start(f32[16,128]{1,0:T(8,128)S(1)} %get-tuple-element.41), channel_id=1, source_target_pairs={{0,32},{32,64},{64,96},{96,128},{128,160},{160,192},{192,224},{224... | collective-permute-start | bytes 24584 | tf_op jit(solution)/shard_map/ppermute | solution.py:360
  52.8 3.8 %collective-permute-start.4 = (f32[16,128]{1,0:T(8,128)S(1)}, f32[16,128]{1,0:T(8,128)S(1)}, u32[]{:S(2)}, u32[]{:S(2)}) collective-permute-start(f32[16,128]{1,0:T(8,128)S(1)} %get-tuple-element.42), channel_id=1, source_target_pairs={{0,224},{32,0},{64,32},{96,64},{128,96},{160,128},{192,160},{224,1... | collective-permute-start | bytes 24584 | tf_op jit(solution)/shard_map/ppermute | solution.py:360
  69.9 3.9 %collective-permute-start.5 = (f32[16,32,128]{2,1,0:T(8,128)S(1)}, f32[16,32,128]{2,1,0:T(8,128)S(1)}, u32[]{:S(2)}, u32[]{:S(2)}) collective-permute-start(f32[16,32,128]{2,1,0:T(8,128)S(1)} %all_to_all.11.mine_new), channel_id=1, source_target_pairs={{0,1},{1,0},{2,3},{3,2},{4,5},{5,4},{6,7},{7,6},{8,9},{9,8},{10,11... | collective-permute-start | bytes 786440 | tf_op jit(solution)/shard_map/ppermute | solution.py:365

commit v2 on v1

--- a/solution.py
+++ b/solution.py
@@ -20,7 +20,7 @@
 SOFT = 0.1
 DT = 0.1
 SPAN = 512
-UNROLL = 8
+UNROLL = 16
 GRANT = 16 * 1024 * 1024
 
 VMEM = pl.BlockSpec(memory_space=pltpu.VMEM)
@@ -141,7 +141,7 @@
 def density_of(cand, own, rho, lists):
     picks = diagonal()
 
-    def one(t, carry):
+    def tile(t):
         listed = [t] + [lists[t, c] for c in range(NBD)]
         other = [[cand[pl.ds(4 * j + k, 8, stride=0), :] for k in range(4)] for j in listed]
         blocks = []
@@ -157,9 +157,13 @@
                 total = part if total is None else total + part
             blocks.append(total)
         rho[pl.ds(t, 1), :] = lane_sums(blocks, picks)
+
+    def one(n, carry):
+        for u in range(2):
+            tile(2 * n + u)
         return carry
 
-    lax.fori_loop(0, TD, one, 0)
+    lax.fori_loop(0, TD // 2, one, 0)
 
 
 def fill_ghosts(cand, below, above):
@@ -229,10 +233,10 @@
                 + (own_rest[rest + 1, rows, :] - vj) * dy
                 + (own_rest[rest + 2, rows, :] - wj) * dz
             )
-            closing = jnp.minimum(closing, 0.0)
             near = d2 + 0.01 * LOG2E
-            bottom = near * near * (own_rest[rest + 4, rows, :] + rj)
-            viscous = closing * (closing - (own_rest[rest + 3, rows, :] + sj) * near) / bottom
+            closing = jnp.minimum(closing, 0.0) / near
+            sound = own_rest[rest + 3, rows, :] + sj
+            viscous = closing * (closing - sound) / (own_rest[rest + 4, rows, :] + rj)
             strength = own_rest[rest + 5, rows, :] + pj + viscous
             weight = strength * jnp.exp2(mj - d2)
             gains[place, rows, :] += weight * dx

time: 92.6 us -> 91.8 us (level)
  no operation moved by 1% of the time
where the time goes in v2:
time: 91.8 us; the launch traced here: 91.6 us
  Pallas kernels  46.2 us (50%)
  blocking collectives  28.4 us (31%)
  starting transfers between devices  14.8 us (16%)
  waiting for transfers between devices  1.38 us (2%)
    all_to_all x2, blocking collectives, sector(): mine = lax.all_to_all(value, 'chip', 0, 0, tiled=True)  28.4 us
    pallas_call x1, Pallas kernels, local(): call(pairs_first, (f32(24, 128), f32(24, 128), f32(24, 128), ghost_rows,...  18.7 us
    pallas_call x1, Pallas kernels, local(): call(pairs_second, (f32(3, 1024), f32(3, 1024), f32(3, 1024), f32(TD, 128...  18.4 us
    ppermute x4, starting transfers between devices, along_space(): lax.ppermute(value, 'space', [(i, (i + steps) % count) for i in range(cou...  9.48 us
    ppermute x2, starting transfers between devices, sector(): return (mine, lax.ppermute(mine, 'core', [(0, 1), (1, 0)]))  5.35 us
    pallas_call x1, Pallas kernels, local(): call(density_first, (f32(CHIPS, 80, 128), f32(TD, 128)), 'vvvvvvsvv', scr...  2.32 us
    pallas_call x1, Pallas kernels, local(): call(density_second, (f32(CHIPS, 32, 128), f32(TD, 128)), 'vvvvvsv', scra...  2.31 us
  transfers between devices with their start and end apart: 6, of which 4 were waited for; matrix products, arithmetic and copies ran while one was open for 0% of the time, Pallas kernels for 4%

profile of v2, /device:TPU:1, one launch (start us, length us, event | category | flops | bytes accessed | tf_op | source)
XLA Modules:
  0.0 91.6 jit_solution(16761257798123387211)
XLA Ops:
  0.6 1.1 %begin.1 = (f32[16,128]{1,0:T(8,128)S(1)}, f32[16,128]{1,0:T(8,128)S(1)}, s32[16,128]{1,0:T(8,128)S(1)}, f32[32,128]{1,0:T(8,128)S(1)}, f32[24,128]{1,0:T(8,128)...) custom-call(f32[3,1024]{1,0:T(4,128)} %pos_in.1, ...), custom_call_target="tpu_custom_call" | custom-call | tf_op jit(solution)/shard_map/begin/pallas_call | solution.py:386
  1.8 2.5 %collective-permute-start = (f32[16,128]{1,0:T(8,128)S(1)}, f32[16,128]{1,0:T(8,128)S(1)}, u32[]{:S(2)}, u32[]{:S(2)}) collective-permute-start(f32[16,128]{1,0:T(8,128)S(1)} %get-tuple-element.31), channel_id=1, source_target_pairs={{0,32},{32,64},{64,96},{96,128},{128,160},{160,192},{192,224},{224... | collective-permute-start | bytes 24584 | tf_op jit(solution)/shard_map/ppermute | solution.py:364
  4.3 4.0 %collective-permute-start.1 = (f32[16,128]{1,0:T(8,128)S(1)}, f32[16,128]{1,0:T(8,128)S(1)}, u32[]{:S(2)}, u32[]{:S(2)}) collective-permute-start(f32[16,128]{1,0:T(8,128)S(1)} %get-tuple-element.32), channel_id=1, source_target_pairs={{0,224},{32,0},{64,32},{96,64},{128,96},{160,128},{192,160},{224,1... | collective-permute-start | bytes 24584 | tf_op jit(solution)/shard_map/ppermute | solution.py:364
  8.3 0.6 places_first.1.own
  9.0 0.3 collective-permute-done.below
  9.3 0.0 collective-permute-done.1.above
  9.3 2.3 %density_first.1 = (f32[16,80,128]{2,1,0:T(8,128)S(1)}, f32[8,128]{1,0:T(8,128)S(1)}) custom-call(f32[24,128]{1,0:T(8,128)S(1)} %get-tuple-element.27.pos, f32[24,128]{1,0:T(8,128)S(1)} %get-tuple-element.28.vel, f32[8,128]{1,0:T(8,128)S(1)} %get-tuple-element.29.mass, f32[8,128]{1,0:T(8,128)S(1)} %get-tuple-element.30.sound2, ...), custom_call_target="tpu_custom_call" | custom-call | tf_op jit(solution)/shard_map/density_first/pallas_call | solution.py:428
  11.6 17.9 %all_to_all.10.mine = f32[16,80,128]{2,1,0:T(8,128)S(1)} all-to-all(f32[16,80,128]{2,1,0:T(8,128)S(1)} %get-tuple-element.35), channel_id=1, replica_groups=mesh['space'=8,'chip'=16,'core'=2] {'chip'}, dimensions={0} | all-to-all | bytes 1310720 | tf_op jit(solution)/shard_map/all_to_all | solution.py:368
  29.5 2.6 %collective-permute-start.2 = (f32[16,80,128]{2,1,0:T(8,128)S(1)}, f32[16,80,128]{2,1,0:T(8,128)S(1)}, u32[]{:S(2)}, u32[]{:S(2)}) collective-permute-start(f32[16,80,128]{2,1,0:T(8,128)S(1)} %all_to_all.10.mine), channel_id=1, source_target_pairs={{0,1},{1,0},{2,3},{3,2},{4,5},{5,4},{6,7},{7,6},{8,9},{9,8},{10,11... | collective-permute-start | bytes 1966088 | tf_op jit(solution)/shard_map/ppermute | solution.py:369
  32.1 1.1 %rest_first.1.own_rest = f32[48,128,128]{2,1,0:T(8,128)S(1)} custom-call(f32[24,128]{1,0:T(8,128)S(1)} %get-tuple-element.28.vel, f32[8,128]{1,0:T(8,128)S(1)} %get-tuple-element.30.sound2, f32[8,128]{1,0:T(8,128)S(1)} %get-tuple-element.38.rho), custom_call_target="tpu_custom_call" | custom-call | tf_op jit(solution)/shard_map/rest_first/pallas_call | solution.py:436
  33.2 0.6 collective-permute-done.2.twin
  33.8 18.7 %pairs_first.1 = (f32[24,128]{1,0:T(8,128)S(1)}, f32[24,128]{1,0:T(8,128)S(1)}, f32[24,128]{1,0:T(8,128)S(1)}, f32[16,128]{1,0:T(8,128)S(1)}, f32[16,128]{1,0:T(8,128)S(1)}) custom-call(f32[16,80,128]{2,1,0:T(8,128)S(1)} %all_to_all.10.mine, f32[16,80,128]{2,1,0:T(8,128)S(1)} %collective-permute-done.2.twin, s32[16,128]{1,0:T(8,128)S(1)} %get-tuple-element.36.codes, ...), custom_call_target="tpu_custom_call" | custom-call | tf_op jit(solution)/shard_map/pairs_first/pallas_call | solution.py:437
  52.5 0.1 collective-permute-start.3
  52.6 2.8 %collective-permute-start.4 = (f32[16,128]{1,0:T(8,128)S(1)}, f32[16,128]{1,0:T(8,128)S(1)}, u32[]{:S(2)}, u32[]{:S(2)}) collective-permute-start(f32[16,128]{1,0:T(8,128)S(1)} %get-tuple-element.42), channel_id=1, source_target_pairs={{0,224},{32,0},{64,32},{96,64},{128,96},{160,128},{192,160},{224,1... | collective-permute-start | bytes 24584 | tf_op jit(solution)/shard_map/ppermute | solution.py:364
  55.4 0.6 places_second.1.own
  56.0 0.3 collective-permute-done.3.below
  56.4 0.0 collective-permute-done.4.above
  56.4 2.3 %density_second.1 = (f32[16,32,128]{2,1,0:T(8,128)S(1)}, f32[8,128]{1,0:T(8,128)S(1)}) custom-call(f32[24,128]{1,0:T(8,128)S(1)} %get-tuple-element.39.pos, f32[8,128]{1,0:T(8,128)S(1)} %get-tuple-element.29.mass, f32[24,128]{1,0:T(8,128)S(1)} %get-tuple-element.40.accel, f32[16,128]{1,0:T(8,128)S(1)} %collective-permute-done.3.below, ...), custom_call_target="tpu_custom_call" | custom-call | tf_op jit(solution)/shard_map/density_second/pallas_call | solution.py:447
  58.7 10.5 %all_to_all.11.mine_new = f32[16,32,128]{2,1,0:T(8,128)S(1)} all-to-all(f32[16,32,128]{2,1,0:T(8,128)S(1)} %get-tuple-element.43), channel_id=1, replica_groups=mesh['space'=8,'chip'=16,'core'=2] {'chip'}, dimensions={0} | all-to-all | bytes 524288 | tf_op jit(solution)/shard_map/all_to_all | solution.py:368
  69.2 2.7 %collective-permute-start.5 = (f32[16,32,128]{2,1,0:T(8,128)S(1)}, f32[16,32,128]{2,1,0:T(8,128)S(1)}, u32[]{:S(2)}, u32[]{:S(2)}) collective-permute-start(f32[16,32,128]{2,1,0:T(8,128)S(1)} %all_to_all.11.mine_new), channel_id=1, source_target_pairs={{0,1},{1,0},{2,3},{3,2},{4,5},{5,4},{6,7},{7,6},{8,9},{9,8},{10,11... | collective-permute-start | bytes 786440 | tf_op jit(solution)/shard_map/ppermute | solution.py:369
  71.9 1.1 %rest_second.1.own_rest = f32[48,128,128]{2,1,0:T(8,128)S(1)} custom-call(f32[24,128]{1,0:T(8,128)S(1)} %get-tuple-element.44.vel, f32[8,128]{1,0:T(8,128)S(1)} %get-tuple-element.30.sound2, f32[8,128]{1,0:T(8,128)S(1)} %get-tuple-element.45.rho), custom_call_target="tpu_custom_call" | custom-call | tf_op jit(solution)/shard_map/rest_second/pallas_call | solution.py:455
  73.0 0.1 collective-permute-done.5.twin_new
  73.1 18.4 %pairs_second.1 = (f32[3,1024]{1,0:T(4,128)}, f32[3,1024]{1,0:T(4,128)}, f32[3,1024]{1,0:T(4,128)}, f32[8,128]{1,0:T(8,128)}) custom-call(f32[16,80,128]{2,1,0:T(8,128)S(1)} %all_to_all.10.mine, f32[16,80,128]{2,1,0:T(8,128)S(1)} %collective-permute-done.2.twin, f32[16,32,128]{2,1,0:T(8,128)S(1)} %all_to_all.11.mine_new, ...), custom_call_target="tpu_custom_call" | custom-call | tf_op jit(solution)/shard_map/pairs_second/pallas_call | solution.py:458
Async XLA Ops:
  1.8 7.5 %collective-permute-start = (f32[16,128]{1,0:T(8,128)S(1)}, f32[16,128]{1,0:T(8,128)S(1)}, u32[]{:S(2)}, u32[]{:S(2)}) collective-permute-start(f32[16,128]{1,0:T(8,128)S(1)} %get-tuple-element.31), channel_id=1, source_target_pairs={{0,32},{32,64},{64,96},{96,128},{128,160},{160,192},{192,224},{224... | collective-permute-start | bytes 24584 | tf_op jit(solution)/shard_map/ppermute | solution.py:364
  4.3 5.0 %collective-permute-start.1 = (f32[16,128]{1,0:T(8,128)S(1)}, f32[16,128]{1,0:T(8,128)S(1)}, u32[]{:S(2)}, u32[]{:S(2)}) collective-permute-start(f32[16,128]{1,0:T(8,128)S(1)} %get-tuple-element.32), channel_id=1, source_target_pairs={{0,224},{32,0},{64,32},{96,64},{128,96},{160,128},{192,160},{224,1... | collective-permute-start | bytes 24584 | tf_op jit(solution)/shard_map/ppermute | solution.py:364
  29.5 4.4 %collective-permute-start.2 = (f32[16,80,128]{2,1,0:T(8,128)S(1)}, f32[16,80,128]{2,1,0:T(8,128)S(1)}, u32[]{:S(2)}, u32[]{:S(2)}) collective-permute-start(f32[16,80,128]{2,1,0:T(8,128)S(1)} %all_to_all.10.mine), channel_id=1, source_target_pairs={{0,1},{1,0},{2,3},{3,2},{4,5},{5,4},{6,7},{7,6},{8,9},{9,8},{10,11... | collective-permute-start | bytes 1966088 | tf_op jit(solution)/shard_map/ppermute | solution.py:369
  52.5 3.9 %collective-permute-start.3 = (f32[16,128]{1,0:T(8,128)S(1)}, f32[16,128]{1,0:T(8,128)S(1)}, u32[]{:S(2)}, u32[]{:S(2)}) collective-permute-start(f32[16,128]{1,0:T(8,128)S(1)} %get-tuple-element.41), channel_id=1, source_target_pairs={{0,32},{32,64},{64,96},{96,128},{128,160},{160,192},{192,224},{224... | collective-permute-start | bytes 24584 | tf_op jit(solution)/shard_map/ppermute | solution.py:364
  52.6 3.8 %collective-permute-start.4 = (f32[16,128]{1,0:T(8,128)S(1)}, f32[16,128]{1,0:T(8,128)S(1)}, u32[]{:S(2)}, u32[]{:S(2)}) collective-permute-start(f32[16,128]{1,0:T(8,128)S(1)} %get-tuple-element.42), channel_id=1, source_target_pairs={{0,224},{32,0},{64,32},{96,64},{128,96},{160,128},{192,160},{224,1... | collective-permute-start | bytes 24584 | tf_op jit(solution)/shard_map/ppermute | solution.py:364
  69.2 3.9 %collective-permute-start.5 = (f32[16,32,128]{2,1,0:T(8,128)S(1)}, f32[16,32,128]{2,1,0:T(8,128)S(1)}, u32[]{:S(2)}, u32[]{:S(2)}) collective-permute-start(f32[16,32,128]{2,1,0:T(8,128)S(1)} %all_to_all.11.mine_new), channel_id=1, source_target_pairs={{0,1},{1,0},{2,3},{3,2},{4,5},{5,4},{6,7},{7,6},{8,9},{9,8},{10,11... | collective-permute-start | bytes 786440 | tf_op jit(solution)/shard_map/ppermute | solution.py:369

commit v3 on v2

--- a/solution.py
+++ b/solution.py
@@ -159,11 +159,11 @@
         rho[pl.ds(t, 1), :] = lane_sums(blocks, picks)
 
     def one(n, carry):
-        for u in range(2):
-            tile(2 * n + u)
+        for u in range(4):
+            tile(4 * n + u)
         return carry
 
-    lax.fori_loop(0, TD // 2, one, 0)
+    lax.fori_loop(0, TD // 4, one, 0)
 
 
 def fill_ghosts(cand, below, above):

time: 91.8 us -> 91.4 us (level)
  no operation moved by 1% of the time
where the time goes in v3:
time: 91.4 us; the launch traced here: 91.2 us
  Pallas kernels  45.8 us (50%)
  blocking collectives  28.3 us (31%)
  starting transfers between devices  14.8 us (16%)
  waiting for transfers between devices  1.38 us (2%)
    all_to_all x2, blocking collectives, sector(): mine = lax.all_to_all(value, 'chip', 0, 0, tiled=True)  28.3 us
    pallas_call x1, Pallas kernels, local(): call(pairs_first, (f32(24, 128), f32(24, 128), f32(24, 128), ghost_rows,...  18.7 us
    pallas_call x1, Pallas kernels, local(): call(pairs_second, (f32(3, 1024), f32(3, 1024), f32(3, 1024), f32(TD, 128...  18.4 us
    ppermute x4, starting transfers between devices, along_space(): lax.ppermute(value, 'space', [(i, (i + steps) % count) for i in range(cou...  9.48 us
    ppermute x2, starting transfers between devices, sector(): return (mine, lax.ppermute(mine, 'core', [(0, 1), (1, 0)]))  5.36 us
    pallas_call x1, Pallas kernels, local(): call(density_first, (f32(CHIPS, 80, 128), f32(TD, 128)), 'vvvvvvsvv', scr...  2.14 us
    pallas_call x1, Pallas kernels, local(): call(density_second, (f32(CHIPS, 32, 128), f32(TD, 128)), 'vvvvvsv', scra...  2.14 us
  transfers between devices with their start and end apart: 6, of which 4 were waited for; matrix products, arithmetic and copies ran while one was open for 0% of the time, Pallas kernels for 4%

profile of v3, /device:TPU:1, one launch (start us, length us, event | category | flops | bytes accessed | tf_op | source)
XLA Modules:
  0.0 91.2 jit_solution(16608938796653061998)
XLA Ops:
  0.6 1.1 %begin.1 = (f32[16,128]{1,0:T(8,128)S(1)}, f32[16,128]{1,0:T(8,128)S(1)}, s32[16,128]{1,0:T(8,128)S(1)}, f32[32,128]{1,0:T(8,128)S(1)}, f32[24,128]{1,0:T(8,128)...) custom-call(f32[3,1024]{1,0:T(4,128)} %pos_in.1, ...), custom_call_target="tpu_custom_call" | custom-call | tf_op jit(solution)/shard_map/begin/pallas_call | solution.py:386
  1.8 2.5 %collective-permute-start = (f32[16,128]{1,0:T(8,128)S(1)}, f32[16,128]{1,0:T(8,128)S(1)}, u32[]{:S(2)}, u32[]{:S(2)}) collective-permute-start(f32[16,128]{1,0:T(8,128)S(1)} %get-tuple-element.31), channel_id=1, source_target_pairs={{0,32},{32,64},{64,96},{96,128},{128,160},{160,192},{192,224},{224... | collective-permute-start | bytes 24584 | tf_op jit(solution)/shard_map/ppermute | solution.py:364
  4.3 4.0 %collective-permute-start.1 = (f32[16,128]{1,0:T(8,128)S(1)}, f32[16,128]{1,0:T(8,128)S(1)}, u32[]{:S(2)}, u32[]{:S(2)}) collective-permute-start(f32[16,128]{1,0:T(8,128)S(1)} %get-tuple-element.32), channel_id=1, source_target_pairs={{0,224},{32,0},{64,32},{96,64},{128,96},{160,128},{192,160},{224,1... | collective-permute-start | bytes 24584 | tf_op jit(solution)/shard_map/ppermute | solution.py:364
  8.3 0.6 places_first.1.own
  9.0 0.3 collective-permute-done.below
  9.3 0.0 collective-permute-done.1.above
  9.3 2.1 %density_first.1 = (f32[16,80,128]{2,1,0:T(8,128)S(1)}, f32[8,128]{1,0:T(8,128)S(1)}) custom-call(f32[24,128]{1,0:T(8,128)S(1)} %get-tuple-element.27.pos, f32[24,128]{1,0:T(8,128)S(1)} %get-tuple-element.28.vel, f32[8,128]{1,0:T(8,128)S(1)} %get-tuple-element.29.mass, f32[8,128]{1,0:T(8,128)S(1)} %get-tuple-element.30.sound2, ...), custom_call_target="tpu_custom_call" | custom-call | tf_op jit(solution)/shard_map/density_first/pallas_call | solution.py:428
  11.4 17.8 %all_to_all.10.mine = f32[16,80,128]{2,1,0:T(8,128)S(1)} all-to-all(f32[16,80,128]{2,1,0:T(8,128)S(1)} %get-tuple-element.35), channel_id=1, replica_groups=mesh['space'=8,'chip'=16,'core'=2] {'chip'}, dimensions={0} | all-to-all | bytes 1310720 | tf_op jit(solution)/shard_map/all_to_all | solution.py:368
  29.3 2.6 %collective-permute-start.2 = (f32[16,80,128]{2,1,0:T(8,128)S(1)}, f32[16,80,128]{2,1,0:T(8,128)S(1)}, u32[]{:S(2)}, u32[]{:S(2)}) collective-permute-start(f32[16,80,128]{2,1,0:T(8,128)S(1)} %all_to_all.10.mine), channel_id=1, source_target_pairs={{0,1},{1,0},{2,3},{3,2},{4,5},{5,4},{6,7},{7,6},{8,9},{9,8},{10,11... | collective-permute-start | bytes 1966088 | tf_op jit(solution)/shard_map/ppermute | solution.py:369
  31.9 1.1 %rest_first.1.own_rest = f32[48,128,128]{2,1,0:T(8,128)S(1)} custom-call(f32[24,128]{1,0:T(8,128)S(1)} %get-tuple-element.28.vel, f32[8,128]{1,0:T(8,128)S(1)} %get-tuple-element.30.sound2, f32[8,128]{1,0:T(8,128)S(1)} %get-tuple-element.38.rho), custom_call_target="tpu_custom_call" | custom-call | tf_op jit(solution)/shard_map/rest_first/pallas_call | solution.py:436
  33.0 0.6 collective-permute-done.2.twin
  33.6 18.7 %pairs_first.1 = (f32[24,128]{1,0:T(8,128)S(1)}, f32[24,128]{1,0:T(8,128)S(1)}, f32[24,128]{1,0:T(8,128)S(1)}, f32[16,128]{1,0:T(8,128)S(1)}, f32[16,128]{1,0:T(8,128)S(1)}) custom-call(f32[16,80,128]{2,1,0:T(8,128)S(1)} %all_to_all.10.mine, f32[16,80,128]{2,1,0:T(8,128)S(1)} %collective-permute-done.2.twin, s32[16,128]{1,0:T(8,128)S(1)} %get-tuple-element.36.codes, ...), custom_call_target="tpu_custom_call" | custom-call | tf_op jit(solution)/shard_map/pairs_first/pallas_call | solution.py:437
  52.3 0.1 collective-permute-start.3
  52.4 2.8 %collective-permute-start.4 = (f32[16,128]{1,0:T(8,128)S(1)}, f32[16,128]{1,0:T(8,128)S(1)}, u32[]{:S(2)}, u32[]{:S(2)}) collective-permute-start(f32[16,128]{1,0:T(8,128)S(1)} %get-tuple-element.42), channel_id=1, source_target_pairs={{0,224},{32,0},{64,32},{96,64},{128,96},{160,128},{192,160},{224,1... | collective-permute-start | bytes 24584 | tf_op jit(solution)/shard_map/ppermute | solution.py:364
  55.2 0.6 places_second.1.own
  55.9 0.3 collective-permute-done.3.below
  56.2 0.0 collective-permute-done.4.above
  56.2 2.1 %density_second.1 = (f32[16,32,128]{2,1,0:T(8,128)S(1)}, f32[8,128]{1,0:T(8,128)S(1)}) custom-call(f32[24,128]{1,0:T(8,128)S(1)} %get-tuple-element.39.pos, f32[8,128]{1,0:T(8,128)S(1)} %get-tuple-element.29.mass, f32[24,128]{1,0:T(8,128)S(1)} %get-tuple-element.40.accel, f32[16,128]{1,0:T(8,128)S(1)} %collective-permute-done.3.below, ...), custom_call_target="tpu_custom_call" | custom-call | tf_op jit(solution)/shard_map/density_second/pallas_call | solution.py:447
  58.3 10.5 %all_to_all.11.mine_new = f32[16,32,128]{2,1,0:T(8,128)S(1)} all-to-all(f32[16,32,128]{2,1,0:T(8,128)S(1)} %get-tuple-element.43), channel_id=1, replica_groups=mesh['space'=8,'chip'=16,'core'=2] {'chip'}, dimensions={0} | all-to-all | bytes 524288 | tf_op jit(solution)/shard_map/all_to_all | solution.py:368
  68.8 2.7 %collective-permute-start.5 = (f32[16,32,128]{2,1,0:T(8,128)S(1)}, f32[16,32,128]{2,1,0:T(8,128)S(1)}, u32[]{:S(2)}, u32[]{:S(2)}) collective-permute-start(f32[16,32,128]{2,1,0:T(8,128)S(1)} %all_to_all.11.mine_new), channel_id=1, source_target_pairs={{0,1},{1,0},{2,3},{3,2},{4,5},{5,4},{6,7},{7,6},{8,9},{9,8},{10,11... | collective-permute-start | bytes 786440 | tf_op jit(solution)/shard_map/ppermute | solution.py:369
  71.5 1.1 %rest_second.1.own_rest = f32[48,128,128]{2,1,0:T(8,128)S(1)} custom-call(f32[24,128]{1,0:T(8,128)S(1)} %get-tuple-element.44.vel, f32[8,128]{1,0:T(8,128)S(1)} %get-tuple-element.30.sound2, f32[8,128]{1,0:T(8,128)S(1)} %get-tuple-element.45.rho), custom_call_target="tpu_custom_call" | custom-call | tf_op jit(solution)/shard_map/rest_second/pallas_call | solution.py:455
  72.6 0.1 collective-permute-done.5.twin_new
  72.7 18.4 %pairs_second.1 = (f32[3,1024]{1,0:T(4,128)}, f32[3,1024]{1,0:T(4,128)}, f32[3,1024]{1,0:T(4,128)}, f32[8,128]{1,0:T(8,128)}) custom-call(f32[16,80,128]{2,1,0:T(8,128)S(1)} %all_to_all.10.mine, f32[16,80,128]{2,1,0:T(8,128)S(1)} %collective-permute-done.2.twin, f32[16,32,128]{2,1,0:T(8,128)S(1)} %all_to_all.11.mine_new, ...), custom_call_target="tpu_custom_call" | custom-call | tf_op jit(solution)/shard_map/pairs_second/pallas_call | solution.py:458
Async XLA Ops:
  1.8 7.5 %collective-permute-start = (f32[16,128]{1,0:T(8,128)S(1)}, f32[16,128]{1,0:T(8,128)S(1)}, u32[]{:S(2)}, u32[]{:S(2)}) collective-permute-start(f32[16,128]{1,0:T(8,128)S(1)} %get-tuple-element.31), channel_id=1, source_target_pairs={{0,32},{32,64},{64,96},{96,128},{128,160},{160,192},{192,224},{224... | collective-permute-start | bytes 24584 | tf_op jit(solution)/shard_map/ppermute | solution.py:364
  4.3 5.0 %collective-permute-start.1 = (f32[16,128]{1,0:T(8,128)S(1)}, f32[16,128]{1,0:T(8,128)S(1)}, u32[]{:S(2)}, u32[]{:S(2)}) collective-permute-start(f32[16,128]{1,0:T(8,128)S(1)} %get-tuple-element.32), channel_id=1, source_target_pairs={{0,224},{32,0},{64,32},{96,64},{128,96},{160,128},{192,160},{224,1... | collective-permute-start | bytes 24584 | tf_op jit(solution)/shard_map/ppermute | solution.py:364
  29.3 4.4 %collective-permute-start.2 = (f32[16,80,128]{2,1,0:T(8,128)S(1)}, f32[16,80,128]{2,1,0:T(8,128)S(1)}, u32[]{:S(2)}, u32[]{:S(2)}) collective-permute-start(f32[16,80,128]{2,1,0:T(8,128)S(1)} %all_to_all.10.mine), channel_id=1, source_target_pairs={{0,1},{1,0},{2,3},{3,2},{4,5},{5,4},{6,7},{7,6},{8,9},{9,8},{10,11... | collective-permute-start | bytes 1966088 | tf_op jit(solution)/shard_map/ppermute | solution.py:369
  52.3 3.9 %collective-permute-start.3 = (f32[16,128]{1,0:T(8,128)S(1)}, f32[16,128]{1,0:T(8,128)S(1)}, u32[]{:S(2)}, u32[]{:S(2)}) collective-permute-start(f32[16,128]{1,0:T(8,128)S(1)} %get-tuple-element.41), channel_id=1, source_target_pairs={{0,32},{32,64},{64,96},{96,128},{128,160},{160,192},{192,224},{224... | collective-permute-start | bytes 24584 | tf_op jit(solution)/shard_map/ppermute | solution.py:364
  52.4 3.8 %collective-permute-start.4 = (f32[16,128]{1,0:T(8,128)S(1)}, f32[16,128]{1,0:T(8,128)S(1)}, u32[]{:S(2)}, u32[]{:S(2)}) collective-permute-start(f32[16,128]{1,0:T(8,128)S(1)} %get-tuple-element.42), channel_id=1, source_target_pairs={{0,224},{32,0},{64,32},{96,64},{128,96},{160,128},{192,160},{224,1... | collective-permute-start | bytes 24584 | tf_op jit(solution)/shard_map/ppermute | solution.py:364
  68.8 3.9 %collective-permute-start.5 = (f32[16,32,128]{2,1,0:T(8,128)S(1)}, f32[16,32,128]{2,1,0:T(8,128)S(1)}, u32[]{:S(2)}, u32[]{:S(2)}) collective-permute-start(f32[16,32,128]{2,1,0:T(8,128)S(1)} %all_to_all.11.mine_new), channel_id=1, source_target_pairs={{0,1},{1,0},{2,3},{3,2},{4,5},{5,4},{6,7},{7,6},{8,9},{9,8},{10,11... | collective-permute-start | bytes 786440 | tf_op jit(solution)/shard_map/ppermute | solution.py:369
